TPU v7x, 32 devices: a whole 2x2x4 slice. The times are simulated.
32 devices in a mesh: dp: 8 (over y, x, core), mp: 4 (over z).
Axes of the slice: x: 2, y: 2, z: 4, core: 2. Of those that a mesh axis runs over, the one named last changes fastest.
Arguments:
- tokens: bfloat16 [2048, 1024], P('dp'), may hold values from -6 to 6
- norm_gain1: float32 [1024], replicated, may hold values from 0.25 to 1.75
- in_weight: bfloat16 [1024, 3, 1024], P(None, None, 'mp'), may hold values from -0.1875 to 0.1875
- conv_taps: float32 [3, 1024], P(None, 'mp'), may hold values from -3 to 3
- out_weight: bfloat16 [1024, 1024], P('mp'), may hold values from -0.1875 to 0.1875
- norm_gain2: float32 [1024], replicated, may hold values from 0.25 to 1.75
- gate_weight: bfloat16 [1024, 4608], P(None, 'mp'), may hold values from -0.1875 to 0.1875
- up_weight: bfloat16 [1024, 4608], P(None, 'mp'), may hold values from -0.1875 to 0.1875
- down_weight: bfloat16 [4608, 1024], P('mp'), may hold values from -0.09375 to 0.09375
- cotangent: bfloat16 [2048, 1024], P('dp'), may hold values from -6 to 6
Outputs:
- block_out: bfloat16 [2048, 1024], P('dp')
- input_grad: bfloat16 [2048, 1024], P('dp')
- grad_gain1: float32 [1024], replicated
- grad_in: float32 [1024, 3, 1024], P('dp', None, 'mp')
- grad_taps: float32 [3, 1024], P(None, 'mp')
- grad_out: float32 [1024, 1024], P('mp', 'dp')
- grad_gain2: float32 [1024], replicated
- grad_gate: float32 [1024, 4608], P('dp', 'mp')
- grad_up: float32 [1024, 4608], P('dp', 'mp')
- grad_down: float32 [4608, 1024], P('mp', 'dp')
All inputs are finite; a program needn't handle non-finite values.
Results may differ from a plain program's by a relative error of at most 0.0098.
Values sent between devices are 32-bit elements; how exact they have to be, the bound alone decides.
A program may use at most 128 MiB of HBM per device.

v0:
```python
import jax
import jax.numpy as jnp
from jax import lax
from jax.sharding import PartitionSpec as P

epsilon = 1e-05


def rms_forward(values, norm_gain):
    inverse = lax.rsqrt(jnp.mean(values * values, axis=-1, keepdims=True) + epsilon)
    unit = values * inverse
    return (unit, inverse, (unit * norm_gain).astype(jnp.bfloat16))


def rms_backward(grad_normed, unit, inverse, norm_gain):
    grad_gain = jnp.sum(grad_normed * unit, axis=0)
    scaled = grad_normed * norm_gain
    grad_values = inverse * (scaled - unit * jnp.mean(scaled * unit, axis=-1, keepdims=True))
    return (grad_values, grad_gain)


def lagged(values, offset):
    return jnp.pad(values, ((offset, 0), (0, 0)))[: values.shape[0]]


def leading(values, offset):
    return jnp.pad(values, ((0, offset), (0, 0)))[offset:]


def conv_forward(mixed, conv_taps):
    total = jnp.zeros(mixed.shape, jnp.float32)
    for offset in range(conv_taps.shape[0]):
        total = total + conv_taps[offset] * lagged(mixed, offset)
    return total


def conv_backward(grad_conv, mixed, conv_taps):
    grad_mixed = jnp.zeros(mixed.shape, jnp.float32)
    rows_list = []
    for offset in range(conv_taps.shape[0]):
        grad_mixed = grad_mixed + conv_taps[offset] * leading(grad_conv, offset)
        rows_list.append(jnp.sum(grad_conv * lagged(mixed, offset), axis=0))
    return (grad_mixed, jnp.stack(rows_list))


def body(
    tokens,
    norm_gain1,
    in_weight,
    conv_taps,
    out_weight,
    norm_gain2,
    gate_weight,
    up_weight,
    down_weight,
    cotangent,
):
    length = tokens.shape[0]
    width = tokens.shape[1]
    in_flat = in_weight.reshape(width, -1)
    streams = in_flat.shape[1]
    inputs = tokens.astype(jnp.float32)
    unit1, inverse1, normed1 = rms_forward(inputs, norm_gain1)
    proj = jnp.dot(normed1, in_flat, preferred_element_type=jnp.float32).reshape(length, 3, -1)
    gate_b = proj[:, 0]
    gate_c = proj[:, 1]
    stream_x = proj[:, 2]
    mixed = gate_b * stream_x
    conved = conv_forward(mixed, conv_taps)
    gated = (gate_c * conved).astype(jnp.bfloat16)
    branch = lax.psum(jnp.dot(gated, out_weight, preferred_element_type=jnp.float32), "mp")
    resid = inputs + branch
    unit2, inverse2, normed2 = rms_forward(resid, norm_gain2)
    gate_pre = jnp.dot(normed2, gate_weight, preferred_element_type=jnp.float32)
    up_pre = jnp.dot(normed2, up_weight, preferred_element_type=jnp.float32)
    sigmoid_gate = jax.nn.sigmoid(gate_pre)
    silu_gate = gate_pre * sigmoid_gate
    hidden = (silu_gate * up_pre).astype(jnp.bfloat16)
    ffn_out = lax.psum(jnp.dot(hidden, down_weight, preferred_element_type=jnp.float32), "mp")
    block_out = (resid + ffn_out).astype(jnp.bfloat16)
    grad_down = jnp.dot(hidden.T, cotangent, preferred_element_type=jnp.float32)
    grad_hidden = jnp.dot(cotangent, down_weight.T, preferred_element_type=jnp.float32)
    grad_gpre = (
        grad_hidden * up_pre * sigmoid_gate * (1.0 + gate_pre * (1.0 - sigmoid_gate))
    ).astype(jnp.bfloat16)
    grad_upre = (grad_hidden * silu_gate).astype(jnp.bfloat16)
    grad_gate = jnp.dot(normed2.T, grad_gpre, preferred_element_type=jnp.float32)
    grad_up = jnp.dot(normed2.T, grad_upre, preferred_element_type=jnp.float32)
    partial_norm2 = jnp.dot(grad_gpre, gate_weight.T, preferred_element_type=jnp.float32) + jnp.dot(
        grad_upre, up_weight.T, preferred_element_type=jnp.float32
    )
    grad_norm2 = lax.psum(partial_norm2, "mp")
    grad_from2, grad_gain2 = rms_backward(grad_norm2, unit2, inverse2, norm_gain2)
    grad_resid = cotangent.astype(jnp.float32) + grad_from2
    resid_bf = grad_resid.astype(jnp.bfloat16)
    grad_out = jnp.dot(gated.T, resid_bf, preferred_element_type=jnp.float32)
    grad_gated = jnp.dot(resid_bf, out_weight.T, preferred_element_type=jnp.float32)
    grad_c = grad_gated * conved
    grad_conv = grad_gated * gate_c
    grad_mixed, grad_taps = conv_backward(grad_conv, mixed, conv_taps)
    grad_proj = (
        jnp.stack([grad_mixed * stream_x, grad_c, grad_mixed * gate_b], axis=1)
        .astype(jnp.bfloat16)
        .reshape(length, streams)
    )
    grad_in = jnp.dot(normed1.T, grad_proj, preferred_element_type=jnp.float32)
    grad_norm1 = lax.psum(jnp.dot(grad_proj, in_flat.T, preferred_element_type=jnp.float32), "mp")
    grad_from1, grad_gain1 = rms_backward(grad_norm1, unit1, inverse1, norm_gain1)
    input_grad = (grad_resid + grad_from1).astype(jnp.bfloat16)
    summed_in, summed_out, summed_gate, summed_up, summed_down = (
        lax.psum_scatter(grad_in, "dp", scatter_dimension=0, tiled=True),
        lax.psum_scatter(grad_out, "dp", scatter_dimension=1, tiled=True),
        lax.psum_scatter(grad_gate, "dp", scatter_dimension=0, tiled=True),
        lax.psum_scatter(grad_up, "dp", scatter_dimension=0, tiled=True),
        lax.psum_scatter(grad_down, "dp", scatter_dimension=1, tiled=True),
    )
    total_gain1, total_taps, total_gain2 = lax.psum((grad_gain1, grad_taps, grad_gain2), "dp")
    return (
        block_out,
        input_grad,
        total_gain1,
        summed_in.reshape(summed_in.shape[0], 3, -1),
        total_taps,
        summed_out,
        total_gain2,
        summed_gate,
        summed_up,
        summed_down,
    )


def solution(mesh):
    in_specs = (
        P("dp", None),
        P(),
        P(None, None, "mp"),
        P(None, "mp"),
        P("mp", None),
        P(),
        P(None, "mp"),
        P(None, "mp"),
        P("mp", None),
        P("dp", None),
    )
    out_specs = (
        P("dp", None),
        P("dp", None),
        P(),
        P("dp", None, "mp"),
        P(None, "mp"),
        P("mp", "dp"),
        P(),
        P("dp", "mp"),
        P("dp", "mp"),
        P("mp", "dp"),
    )
    return jax.shard_map(body, mesh=mesh, in_specs=in_specs, out_specs=out_specs, check_vma=False)
```

profile of v0, /device:TPU:0, one launch (start us, length us, event | category | flops | bytes accessed | tf_op | source)
XLA Modules:
  0.0 491.8 jit_solution(12263484071148346959)
XLA Ops:
  7.3 2.7 copy.21
  10.2 2.1 fusion
  14.0 1.3 fusion.32
  15.4 54.7 %all-reduce.10.cloned.1.call-done = f32[256,1024]{1,0:T(8,128)} async-done(((f32[256,1024]{1,0:T(8,128)}), f32[256,1024]{1,0:T(8,128)}) %all-reduce.10.cloned.1.call-update) | async-done | bytes 1048592 | tf_op jit(solution)/shard_map/psum | solution.py:71
  70.1 1.7 multiply_reduce_fusion.2
  72.3 0.9 fusion.33
  73.2 1.0 copy-done.4
  75.2 2.1 multiply_convert_fusion
  78.3 1.9 convolution_add_fusion
  80.3 2.9 fusion.35
  83.2 48.3 %all-reduce.12.cloned.1.call-done = f32[256,1024]{1,0:T(8,128)} async-done(((f32[256,1024]{1,0:T(8,128)}), f32[256,1024]{1,0:T(8,128)}) %all-reduce.12.cloned.1.call-update) | async-done | bytes 1048592 | tf_op jit(solution)/shard_map/psum | solution.py:92
  131.5 1.7 multiply_reduce_fusion
  134.6 0.9 multiply_reduce_fusion.5
  136.5 1.6 convolution_bitcast_fusion
  138.2 1.8 maximum_convert_fusion
  139.9 1.9 copy.22
  141.8 3.6 fusion.26
  146.3 2.5 fusion.20
  148.9 4.3 fusion.37
  153.3 4.3 fusion.38
  157.7 4.3 fusion.39
  162.6 61.1 %all-reduce.14.cloned.1.call-done = (f32[256,1024]{1,0:T(8,128)}, f32[256,1024]{1,0:T(8,128)}) async-done(((f32[256,1024]{1,0:T(8,128)}, f32[256,1024]{1,0:T(8,128)}), (f32[256,1024]{1,0:T(8,128)}, f32[256,1024]{1,0:T(8,128)})) %all-reduce.14.cloned.1.call-update) | async-done | bytes 2097168 | tf_op jit(solution)/shard_map/psum | solution.py:79
  223.7 1.8 fusion.13
  225.5 23.6 %all-reduce.4 = (f32[1024]{0:T(1024)}, f32[3,256]{1,0:T(4,128)}, f32[1024]{0:T(1024)}) all-reduce(f32[1024]{0:T(1024)S(1)} %get-tuple-element.32, f32[3,256]{1,0:T(4,128)S(1)} %pad_maximum_fusion, f32[1024]{0:T(1024)S(1)} %get-tuple-element.30), channel_id=1, replica_groups=mesh['dp'=8,'mp'=4] {'dp'}, use_global_device_ids=true, to_apply=%region_9.10 | all-reduce | flops 2816 | bytes 22528 | tf_op jit(solution)/shard_map/psum | solution.py:117
  249.2 3.3 fusion.12
  252.5 19.7 %reduce-scatter.6.cloned.1.call-done = f32[128,768]{1,0:T(8,128)} async-done(((f32[1024,768]{1,0:T(8,128)}), f32[128,768]{1,0:T(8,128)}) %reduce-scatter.6.cloned.1.call-update) | async-done | bytes 393232 | tf_op jit(solution)/shard_map/reduce_scatter | solution.py:111
  272.1 1.1 copy.23
  273.3 0.9 copy.24
  274.2 37.5 %reduce-scatter.8.cloned.1.call-done = f32[256,128]{1,0:T(8,128)} async-done(((f32[256,1024]{1,0:T(8,128)}), f32[256,128]{1,0:T(8,128)}) %reduce-scatter.8.cloned.1.call-update) | async-done | bytes 131088 | tf_op jit(solution)/shard_map/reduce_scatter | solution.py:112
  311.7 57.7 %reduce-scatter.10.cloned.1.call-done = f32[128,1152]{1,0:T(8,128)} async-done(((f32[1024,1152]{1,0:T(8,128)}), f32[128,1152]{1,0:T(8,128)}) %reduce-scatter.10.cloned.1.call-update) | async-done | bytes 589840 | tf_op jit(solution)/shard_map/reduce_scatter | solution.py:113
  369.4 57.8 %reduce-scatter.12.cloned.1.call-done = f32[128,1152]{1,0:T(8,128)} async-done(((f32[1024,1152]{1,0:T(8,128)}), f32[128,1152]{1,0:T(8,128)}) %reduce-scatter.12.cloned.1.call-update) | async-done | bytes 589840 | tf_op jit(solution)/shard_map/reduce_scatter | solution.py:114
  427.2 57.7 %reduce-scatter.14.cloned.1.call-done = f32[1152,128]{1,0:T(8,128)} async-done(((f32[1152,1024]{1,0:T(8,128)}), f32[1152,128]{1,0:T(8,128)}) %reduce-scatter.14.cloned.1.call-update) | async-done | bytes 589840 | tf_op jit(solution)/shard_map/reduce_scatter | solution.py:115
  (87 shorter events, 8.4 us)
Async XLA Ops:
  7.2 67.8 %copy-start = (bf16[1152,1024]{1,0:T(8,128)(2,1)S(1)}, bf16[1152,1024]{1,0:T(8,128)(2,1)}, u32[]{:S(2)}) copy-start(bf16[1152,1024]{1,0:T(8,128)(2,1)} %param.18) | copy-start | bytes 7077892
  7.2 2.8 copy-start.3
  7.2 3.0 copy-start.24
  7.2 62.9 %all-reduce.10.cloned.1.call-start = ((), (), s32[]{:S(2)}) async-start(), calls=%async_computation.5 | async-start | bytes 2097152 | tf_op jit(solution)/shard_map/psum | solution.py:71
  10.0 2.4 copy-start.27
  10.2 3.8 copy-start.16
  12.3 0.9 copy-start.8
  12.4 3.0 copy-start.12
  14.0 1.4 copy-start.20
  14.0 57.9 %copy-start.23 = (f32[1024]{0:T(1024)S(1)}, f32[1024]{0:T(1024)}, u32[]{:S(2)}) copy-start(f32[1024]{0:T(1024)} %param.15) | copy-start | bytes 12292
  15.3 116.2 %all-reduce.12.cloned.1.call-start = ((), (), s32[]{:S(2)}) async-start(), calls=%async_computation.6 | async-start | bytes 2097152 | tf_op jit(solution)/shard_map/psum | solution.py:92
  70.1 2.1 copy-start.5
  72.3 0.9 copy-start.1
  72.3 1.9 copy-start.4
  74.1 1.0 copy-start.14
  77.3 0.9 copy-start.11
  77.3 1.0 copy-start.10
  80.2 143.5 %all-reduce.14.cloned.1.call-start = ((), (), s32[]{:S(2)}) async-start(), calls=%async_computation.12 | async-start | bytes 4194304 | tf_op jit(solution)/shard_map/psum | solution.py:79
  131.5 1.8 copy-start.7
  131.5 1.8 copy-start.15
  133.2 1.1 copy-start.9
  133.3 1.2 copy-start.13
  133.3 1.3 copy-start.17
  134.6 1.2 copy-start.2
  134.6 1.1 copy-start.22
  134.6 1.9 copy-start.6
  138.1 134.0 %reduce-scatter.6.cloned.1.call-start = ((), (), s32[]{:S(2)}) async-start(), calls=%async_computation.7 | async-start | bytes 3538944 | tf_op jit(solution)/shard_map/reduce_scatter | solution.py:111
  145.4 0.9 copy-start.21
  145.5 166.2 %reduce-scatter.8.cloned.1.call-start = ((), (), s32[]{:S(2)}) async-start(), calls=%async_computation.8 | async-start | bytes 1179648 | tf_op jit(solution)/shard_map/reduce_scatter | solution.py:112
  148.9 220.5 %reduce-scatter.10.cloned.1.call-start = ((), (), s32[]{:S(2)}) async-start(), calls=%async_computation.9 | async-start | bytes 5308416 | tf_op jit(solution)/shard_map/reduce_scatter | solution.py:113
  153.2 274.0 %reduce-scatter.12.cloned.1.call-start = ((), (), s32[]{:S(2)}) async-start(), calls=%async_computation.10 | async-start | bytes 5308416 | tf_op jit(solution)/shard_map/reduce_scatter | solution.py:114
  157.6 327.3 %reduce-scatter.14.cloned.1.call-start = ((), (), s32[]{:S(2)}) async-start(), calls=%async_computation.11 | async-start | bytes 5308416 | tf_op jit(solution)/shard_map/reduce_scatter | solution.py:115
  (4 other events, 2.7 us)
Sparse Core Ops, SparseCore 0:
  15.5 54.6 all-reduce.9
  80.3 51.1 all-reduce.11
  138.2 85.4 all-reduce.13
  227.0 45.1 reduce-scatter.5
  275.7 35.9 reduce-scatter.7
  315.6 53.7 reduce-scatter.9
  373.4 53.7 reduce-scatter.11
  431.2 53.6 reduce-scatter.13
where the time goes:
time: 492 us
  waiting for transfers between devices  395 us (80%)
  matrix products  34.4 us (7%)
  blocking collectives  23.6 us (5%)
  between operations  14.4 us (3%)
  local copies, waits for them, and re-layouts  12.3 us (2%)
  other arithmetic  12 us (2%)
    psum x1, waiting for transfers between devices, body(): lax.psum(jnp.dot(hidden, down_weight, preferred_element_type=jnp.float32)...  61.1 us
    reduce_scatter x1, waiting for transfers between devices, body(): lax.psum_scatter(grad_up, 'dp', scatter_dimension=0, tiled=True)  57.8 us
    reduce_scatter x1, waiting for transfers between devices, body(): lax.psum_scatter(grad_down, 'dp', scatter_dimension=1, tiled=True)  57.7 us
    reduce_scatter x1, waiting for transfers between devices, body(): lax.psum_scatter(grad_gate, 'dp', scatter_dimension=0, tiled=True)  57.7 us
    psum x1, waiting for transfers between devices, body(): lax.psum(jnp.dot(gated, out_weight, preferred_element_type=jnp.float32),...  54.7 us
    psum x1, waiting for transfers between devices, body(): grad_norm2 = lax.psum(partial_norm2, 'mp')  48.3 us
    reduce_scatter x1, waiting for transfers between devices, body(): lax.psum_scatter(grad_out, 'dp', scatter_dimension=1, tiled=True)  37.5 us
    psum x1, blocking collectives, body(): lax.psum((grad_gain1, grad_taps, grad_gain2), 'dp')  23.6 us
  transfers between devices with their start and end apart: 8, of which 8 were waited for; matrix products, arithmetic and copies ran while one was open for 7% of the time, Pallas kernels for 0%

commit v1 on v0

--- a/solution.py
+++ b/solution.py
@@ -76,7 +76,10 @@
     sigmoid_gate = jax.nn.sigmoid(gate_pre)
     silu_gate = gate_pre * sigmoid_gate
     hidden = (silu_gate * up_pre).astype(jnp.bfloat16)
-    ffn_out = lax.psum(jnp.dot(hidden, down_weight, preferred_element_type=jnp.float32), "mp")
+    ffn_out = jnp.sum(
+        lax.all_gather(jnp.dot(hidden, down_weight, preferred_element_type=jnp.float32), "mp"),
+        axis=0,
+    )
     block_out = (resid + ffn_out).astype(jnp.bfloat16)
     grad_down = jnp.dot(hidden.T, cotangent, preferred_element_type=jnp.float32)
     grad_hidden = jnp.dot(cotangent, down_weight.T, preferred_element_type=jnp.float32)

time: 492 us -> 545 us (1.11)
  waiting for transfers between devices: 395 us -> 441 us
  other arithmetic: 12 us -> 19.1 us
    all_gather x0 -> x1, waiting for transfers between devices: none -> 79.7 us  [body(): lax.all_gather(jnp.dot(hidden, down_weight, preferred_element_type=jnp.fl...]
    psum x1, waiting for transfers between devices: 61.1 us -> 27.1 us  [body(): lax.psum(jnp.dot(grad_proj, in_flat.T, preferred_element_type=jnp.float32...]
  transfers between devices with their start and end apart: 8 -> 9, of which waited for: 8 -> 9; matrix products, arithmetic and copies ran while one was open for 7% -> 6% of each run, Pallas kernels for 0% -> 0%
where the time goes in v1:
time: 545 us; the launch traced here: 544 us
  waiting for transfers between devices  441 us (81%)
  matrix products  33.8 us (6%)
  blocking collectives  24.1 us (4%)
  other arithmetic  19.1 us (4%)
  between operations  14.1 us (3%)
  local copies, waits for them, and re-layouts  11 us (2%)
    all_gather x1, waiting for transfers between devices, body(): lax.all_gather(jnp.dot(hidden, down_weight, preferred_element_type=jnp.fl...  79.7 us
    reduce_scatter x1, waiting for transfers between devices, body(): lax.psum_scatter(grad_up, 'dp', scatter_dimension=0, tiled=True)  57.8 us
    reduce_scatter x1, waiting for transfers between devices, body(): lax.psum_scatter(grad_gate, 'dp', scatter_dimension=0, tiled=True)  57.8 us
    reduce_scatter x1, waiting for transfers between devices, body(): lax.psum_scatter(grad_down, 'dp', scatter_dimension=1, tiled=True)  55.5 us
    psum x1, waiting for transfers between devices, body(): lax.psum(jnp.dot(gated, out_weight, preferred_element_type=jnp.float32),...  54.7 us
    psum x1, waiting for transfers between devices, body(): grad_norm2 = lax.psum(partial_norm2, 'mp')  48.3 us
    reduce_scatter x1, waiting for transfers between devices, body(): lax.psum_scatter(grad_out, 'dp', scatter_dimension=1, tiled=True)  39.8 us
    psum x1, waiting for transfers between devices, body(): lax.psum(jnp.dot(grad_proj, in_flat.T, preferred_element_type=jnp.float32...  27.1 us
  transfers between devices with their start and end apart: 9, of which 9 were waited for; matrix products, arithmetic and copies ran while one was open for 6% of the time, Pallas kernels for 0%

profile of v1, /device:TPU:0, one launch (start us, length us, event | category | flops | bytes accessed | tf_op | source)
XLA Modules:
  0.0 543.7 jit_solution(18265309840009982418)
XLA Ops:
  7.3 1.4 fusion.14
  9.5 2.6 copy.21
  12.0 2.1 fusion
  15.9 1.3 fusion.32
  17.3 54.7 %all-reduce.9.cloned.1.call-done = f32[256,1024]{1,0:T(8,128)} async-done(((f32[256,1024]{1,0:T(8,128)}), f32[256,1024]{1,0:T(8,128)}) %all-reduce.9.cloned.1.call-update) | async-done | bytes 1048592 | tf_op jit(solution)/shard_map/psum | solution.py:71
  72.0 1.6 multiply_reduce_fusion.2
  76.7 2.1 multiply_convert_fusion
  79.8 1.9 convolution_add_fusion
  81.8 2.9 fusion.35
  84.8 48.3 %all-reduce.11.cloned.1.call-done = f32[256,1024]{1,0:T(8,128)} async-done(((f32[256,1024]{1,0:T(8,128)}), f32[256,1024]{1,0:T(8,128)}) %all-reduce.11.cloned.1.call-update) | async-done | bytes 1048592 | tf_op jit(solution)/shard_map/psum | solution.py:95
  133.0 1.9 multiply_reduce_fusion
  134.9 79.7 %all-gather.3.cloned.1.call-done = f32[1024,1024]{1,0:T(8,128)} async-done(((f32[256,1024]{1,0:T(8,128)}), f32[1024,1024]{1,0:T(8,128)}) %all-gather.3.cloned.1.call-update) | async-done | bytes 4194320 | tf_op jit(solution)/shard_map/all_gather | solution.py:80
  214.6 3.7 reduce_sum.92
  218.3 3.3 multiply_add_fusion
  223.5 1.6 convolution_bitcast_fusion
  225.2 1.8 maximum_convert_fusion
  226.9 1.9 copy.22
  228.8 3.3 fusion.26
  232.2 4.3 fusion.39
  236.6 4.1 fusion.38
  241.0 4.1 fusion.37
  246.0 2.5 fusion.20
  248.6 27.1 %all-reduce.13.cloned.1.call-done = f32[256,1024]{1,0:T(8,128)} async-done(((f32[256,1024]{1,0:T(8,128)}), f32[256,1024]{1,0:T(8,128)}) %all-reduce.13.cloned.1.call-update) | async-done | bytes 1048592 | tf_op jit(solution)/shard_map/psum | solution.py:110
  275.6 1.7 fusion.13
  277.3 24.1 %all-reduce.4 = (f32[1024]{0:T(1024)}, f32[3,256]{1,0:T(4,128)}, f32[1024]{0:T(1024)}) all-reduce(f32[1024]{0:T(1024)S(1)} %get-tuple-element.32, f32[3,256]{1,0:T(4,128)S(1)} %pad_maximum_fusion, f32[1024]{0:T(1024)S(1)} %get-tuple-element.30), channel_id=1, replica_groups=mesh['dp'=8,'mp'=4] {'dp'}, use_global_device_ids=true, to_apply=%region_9.10 | all-reduce | flops 2816 | bytes 22528 | tf_op jit(solution)/shard_map/psum | solution.py:120
  301.4 2.6 fusion.12
  304.0 20.2 %reduce-scatter.6.cloned.1.call-done = f32[128,768]{1,0:T(8,128)} async-done(((f32[1024,768]{1,0:T(8,128)}), f32[128,768]{1,0:T(8,128)}) %reduce-scatter.6.cloned.1.call-update) | async-done | bytes 393232 | tf_op jit(solution)/shard_map/reduce_scatter | solution.py:114
  324.2 1.1 copy.23
  326.3 55.5 %reduce-scatter.14.cloned.1.call-done = f32[1152,128]{1,0:T(8,128)} async-done(((f32[1152,1024]{1,0:T(8,128)}), f32[1152,128]{1,0:T(8,128)}) %reduce-scatter.14.cloned.1.call-update) | async-done | bytes 589840 | tf_op jit(solution)/shard_map/reduce_scatter | solution.py:118
  381.8 57.8 %reduce-scatter.12.cloned.1.call-done = f32[128,1152]{1,0:T(8,128)} async-done(((f32[1024,1152]{1,0:T(8,128)}), f32[128,1152]{1,0:T(8,128)}) %reduce-scatter.12.cloned.1.call-update) | async-done | bytes 589840 | tf_op jit(solution)/shard_map/reduce_scatter | solution.py:117
  439.6 57.8 %reduce-scatter.10.cloned.1.call-done = f32[128,1152]{1,0:T(8,128)} async-done(((f32[1024,1152]{1,0:T(8,128)}), f32[128,1152]{1,0:T(8,128)}) %reduce-scatter.10.cloned.1.call-update) | async-done | bytes 589840 | tf_op jit(solution)/shard_map/reduce_scatter | solution.py:116
  497.5 39.8 %reduce-scatter.8.cloned.1.call-done = f32[256,128]{1,0:T(8,128)} async-done(((f32[256,1024]{1,0:T(8,128)}), f32[256,128]{1,0:T(8,128)}) %reduce-scatter.8.cloned.1.call-update) | async-done | bytes 131088 | tf_op jit(solution)/shard_map/reduce_scatter | solution.py:115
  (85 shorter events, 10.8 us)
Async XLA Ops:
  7.2 69.3 %copy-start = (bf16[1152,1024]{1,0:T(8,128)(2,1)S(1)}, bf16[1152,1024]{1,0:T(8,128)(2,1)}, u32[]{:S(2)}) copy-start(bf16[1152,1024]{1,0:T(8,128)(2,1)} %param.18) | copy-start | bytes 7077892
  7.2 4.8 copy-start.3
  7.2 4.8 copy-start.22
  7.2 64.8 %all-reduce.9.cloned.1.call-start = ((), (), s32[]{:S(2)}) async-start(), calls=%async_computation.5 | async-start | bytes 2097152 | tf_op jit(solution)/shard_map/psum | solution.py:71
  12.0 3.8 copy-start.13
  14.1 0.9 copy-start.7
  14.2 59.4 %copy-start.11 = (f32[256,256]{1,0:T(8,128)}, f32[256,256]{1,0:T(8,128)S(1)}, u32[]{:S(2)}) copy-start(f32[256,256]{1,0:T(8,128)S(1)} %fusion.25) | copy-start | bytes 786436
  15.9 57.7 %copy-start.18 = (bf16[256,256]{1,0:T(8,128)(2,1)}, bf16[256,256]{1,0:T(8,128)(2,1)S(1)}, u32[]{:S(2)}) copy-start(bf16[256,256]{1,0:T(8,128)(2,1)S(1)} %get-tuple-element.45) | copy-start | bytes 393220
  15.9 57.8 %copy-start.21 = (f32[1024]{0:T(1024)S(1)}, f32[1024]{0:T(1024)}, u32[]{:S(2)}) copy-start(f32[1024]{0:T(1024)} %param.15) | copy-start | bytes 12292
  17.2 115.8 %all-reduce.11.cloned.1.call-start = ((), (), s32[]{:S(2)}) async-start(), calls=%async_computation.6 | async-start | bytes 2097152 | tf_op jit(solution)/shard_map/psum | solution.py:95
  72.0 2.0 copy-start.4
  73.6 1.2 copy-start.1
  74.0 1.7 copy-start.5
  75.6 1.0 copy-start.15
  78.8 0.9 copy-start.10
  78.8 1.0 copy-start.9
  81.7 132.9 %all-gather.3.cloned.1.call-start = ((), (), s32[]{:S(2)}) async-start(), calls=%async_computation.13 | async-start | bytes 5242880 | tf_op jit(solution)/shard_map/all_gather | solution.py:80
  84.7 190.9 %all-reduce.13.cloned.1.call-start = ((), (), s32[]{:S(2)}) async-start(), calls=%async_computation.7 | async-start | bytes 2097152 | tf_op jit(solution)/shard_map/psum | solution.py:110
  218.3 3.3 copy-start.8
  218.3 3.3 copy-start.12
  218.3 3.3 copy-start.14
  221.6 1.2 copy-start.2
  221.6 1.1 copy-start.20
  221.6 1.8 copy-start.6
  225.1 99.1 %reduce-scatter.6.cloned.1.call-start = ((), (), s32[]{:S(2)}) async-start(), calls=%async_computation.8 | async-start | bytes 3538944 | tf_op jit(solution)/shard_map/reduce_scatter | solution.py:114
  232.2 149.6 %reduce-scatter.14.cloned.1.call-start = ((), (), s32[]{:S(2)}) async-start(), calls=%async_computation.12 | async-start | bytes 5308416 | tf_op jit(solution)/shard_map/reduce_scatter | solution.py:118
  236.5 203.1 %reduce-scatter.12.cloned.1.call-start = ((), (), s32[]{:S(2)}) async-start(), calls=%async_computation.11 | async-start | bytes 5308416 | tf_op jit(solution)/shard_map/reduce_scatter | solution.py:117
  240.7 256.7 %reduce-scatter.10.cloned.1.call-start = ((), (), s32[]{:S(2)}) async-start(), calls=%async_computation.10 | async-start | bytes 5308416 | tf_op jit(solution)/shard_map/reduce_scatter | solution.py:116
  245.1 0.9 copy-start.19
  245.1 3.4 copy-start.23
  245.1 3.4 copy-start.24
  245.1 292.1 %reduce-scatter.8.cloned.1.call-start = ((), (), s32[]{:S(2)}) async-start(), calls=%async_computation.9 | async-start | bytes 1179648 | tf_op jit(solution)/shard_map/reduce_scatter | solution.py:115
  (2 other events, 1.3 us)
Sparse Core Ops, SparseCore 0:
  17.3 54.6 all-reduce.8
  81.8 51.1 all-reduce.10
  134.6 79.9 all-gather.2
  225.2 50.3 all-reduce.12
  278.9 45.3 reduce-scatter.5
  328.1 53.6 reduce-scatter.13
  385.8 53.7 reduce-scatter.11
  443.6 53.7 reduce-scatter.9
  501.2 35.9 reduce-scatter.7
